TPU v7x, 32 devices: a whole 2x2x4 slice. The times are simulated.
32 devices in a mesh: fiber: 8 (over z, core), group: 4 (over y, x).
Axes of the slice: x: 2, y: 2, z: 4, core: 2. Of those that a mesh axis runs over, the one named last changes fastest.
Arguments:
- field_slab: float32 [512, 64, 2048], P('fiber', 'group'), may hold values from -42 to 42
- start_basis: float32 [512, 128], replicated, may hold values from -6 to 6
Outputs:
- factor: float32 [512, 128], replicated
- core_slab: float32 [128, 64, 2048], P(None, 'group', 'fiber')
All inputs are finite; a program needn't handle non-finite values.
Results may differ from a plain program's by a relative error of at most 0.0003.
Values sent between devices are 32-bit elements; how exact they have to be, the bound alone decides.
No kernel may reach another device: no remote copies, remote signals or barrier semaphores. Data moves between devices by JAX's collectives and lax.ppermute only.
A program may use at most 128 MiB of HBM per device.

v0:
```python
import jax
import jax.numpy as jnp
from jax import lax
from jax.sharding import PartitionSpec as P

ITERS = 2
precise = lax.Precision.HIGHEST


def orthonormal(images):
    inner_products = jnp.dot(images.T, images, precision=precise)
    cholesky_factor = jnp.linalg.cholesky(inner_products)
    return lax.linalg.triangular_solve(
        cholesky_factor, images, left_side=False, lower=True, transpose_a=True
    )


def on_device(field_slab, start_basis):
    column_count = field_slab.shape[1] * field_slab.shape[2] * lax.axis_size("group")
    regrouped = lax.all_to_all(field_slab, "fiber", split_axis=2, concat_axis=0, tiled=True)
    columns = regrouped.reshape(regrouped.shape[0], regrouped.shape[1] * regrouped.shape[2])
    local_gram = jnp.dot(columns, columns.T, precision=precise)
    subspace = start_basis
    fiber_share = lax.psum_scatter(local_gram, "fiber", scatter_dimension=0, tiled=True)
    gram_share = lax.psum(fiber_share, "group") / column_count
    for iteration in range(ITERS):
        image_rows = jnp.dot(gram_share, subspace, precision=precise)
        subspace = orthonormal(lax.all_gather(image_rows, "fiber", axis=0, tiled=True))
    core_slab = jnp.einsum("mk,mbc->kbc", subspace, regrouped, precision=precise)
    return (subspace, core_slab)


def solution(mesh):
    return jax.shard_map(
        on_device,
        mesh=mesh,
        in_specs=(P("fiber", "group", None), P()),
        out_specs=(P(), P(None, "group", "fiber")),
        check_vma=False,
    )
```

profile of v0, /device:TPU:0, one launch (start us, length us, event | category | flops | bytes accessed | tf_op | source)
XLA Modules:
  0.0 485.6 jit_solution(11098625435497381214)
XLA Ops:
  7.2 15.6 %copy.22 = f32[64,16,2048]{0,1,2:T(8,128)} copy(f32[64,16,2048]{2,1,0:T(8,128)} %param.5) | data formatting | bytes 16777216 | tf_op args[0]
  22.8 15.4 %reshape.27 = f32[8,1,262144]{2,1,0:T(1,128)} reshape(f32[2048,16,64]{2,1,0:T(8,128)} %bitcast.49) | data formatting | bytes 16777216
  38.2 190.7 %all_to_all.18 = f32[8,1,262144]{2,1,0:T(1,128)} all-to-all(f32[8,1,262144]{2,1,0:T(1,128)} %reshape.27), channel_id=1, replica_groups=mesh['fiber'=8,'group'=4] {'fiber'}, dimensions={0} | all-to-all | bytes 16777216 | tf_op jit(solution)/shard_map/all_to_all | solution.py:20
  228.9 0.5 broadcast.36
  229.4 26.2 %reduce.4 = f32[8,262144]{1,0:T(8,128)} reduce(f32[8,1,262144]{2,1,0:T(1,128)} %all_to_all.18, f32[]{:T(128)} %broadcast.36), dimensions={1}, to_apply=%all_to_all.13.reduce_sub_computation | reduce | bytes 16777220 | tf_op jit(solution)/shard_map/all_to_all | solution.py:20
  255.7 15.6 %reshape.28 = f32[2048,16,64]{2,1,0:T(8,128)} reshape(f32[8,262144]{1,0:T(8,128)} %reduce.4) | data formatting | bytes 16777216
  271.3 15.8 %copy.23 = f32[64,16,8,256]{3,1,0,2:T(8,128)} copy(f32[64,16,8,256]{0,1,3,2:T(8,128)} %bitcast.47) | data formatting | bytes 16777216 | tf_op jit(solution)/shard_map/all_to_all | solution.py:20
  287.0 11.5 %copy.30 = f32[64,8,16,256]{3,1,2,0:T(8,128)S(1)} copy(f32[64,8,16,256]{3,2,1,0:T(8,128)} %bitcast.51) | data formatting | bytes 16777216
  298.5 14.9 %fusion.19 = f32[512,512]{1,0:T(8,128)} fusion(f32[512,4096]{1,0:T(8,128)S(1)} %bitcast.46), kind=kOutput, calls=%fused_computation.29 | convolution fusion | flops 12884901888 | bytes 9437184 | tf_op jit(solution)/shard_map/dot_general | solution.py:22
  313.5 32.2 %reduce-scatter.2.cloned.1.call-done = f32[64,512]{1,0:T(8,128)} async-done(((f32[512,512]{1,0:T(8,128)}), f32[64,512]{1,0:T(8,128)}) %reduce-scatter.2.cloned.1.call-update) | async-done | bytes 131088 | tf_op jit(solution)/shard_map/reduce_scatter | solution.py:24
  345.7 12.8 %copy.26 = f32[8,64,16,256]{3,1,0,2:T(8,128)} copy(f32[8,64,16,256]{1,2,3,0:T(8,128)} %bitcast.48) | data formatting | bytes 16777216 | tf_op jit(solution)/shard_map/all_to_all | solution.py:20
  358.5 30.5 %all-reduce.2.cloned.1.call-done = f32[64,512]{1,0:T(8,128)} async-done(((f32[64,512]{1,0:T(8,128)}), f32[64,512]{1,0:T(8,128)}) %all-reduce.2.cloned.1.call-update) | async-done | bytes 131088 | tf_op jit(solution)/shard_map/psum | solution.py:25
  389.0 1.2 fusion.4
  390.2 14.3 %all_gather.6 = f32[512,128]{1,0:T(8,128)S(1)} all-gather(f32[64,128]{1,0:T(8,128)S(1)} %fusion.4), channel_id=1, replica_groups=mesh['fiber'=8,'group'=4] {'fiber'}, dimensions={0}, use_global_device_ids=true | all-gather | bytes 294912 | tf_op jit(solution)/shard_map/all_gather | solution.py:28
  404.5 0.6 fusion.20
  405.2 11.7 %cholesky.44 = f32[128,128]{1,0:T(8,128)S(1)} custom-call(f32[128,128]{1,0:T(8,128)S(1)} %fusion.12), custom_call_target="Cholesky" | custom-call | tf_op jit(solution)/shard_map/jit(cholesky)/cholesky | solution.py:12
  416.9 0.6 compare_reduce_fusion.1
  417.6 0.7 fusion.6
  418.2 9.8 %custom-call.6 = f32[1,128,128]{1,2,0:T(8,128)S(1)} custom-call(f32[1,128,128]{2,1,0:T(8,128)S(1)} %fusion.6), custom_call_target="InvertDiagBlocksLowerTriangular" | custom-call | tf_op jit(solution)/shard_map/triangular_solve/custom-call.0 | solution.py:13
  428.0 0.4 convolution_bitcast_fusion
  428.5 1.3 fusion.2
  429.8 14.4 %all_gather.7 = f32[512,128]{1,0:T(8,128)S(1)} all-gather(f32[64,128]{1,0:T(8,128)S(1)} %fusion.2), channel_id=1, replica_groups=mesh['fiber'=8,'group'=4] {'fiber'}, dimensions={0}, use_global_device_ids=true | all-gather | bytes 294912 | tf_op jit(solution)/shard_map/all_gather | solution.py:28
  444.2 0.6 fusion.21
  444.8 0.1 copy.25
  444.9 11.7 %cholesky.55 = f32[128,128]{1,0:T(8,128)S(1)} custom-call(f32[128,128]{1,0:T(8,128)S(1)} %fusion.10), custom_call_target="Cholesky" | custom-call | tf_op jit(solution)/shard_map/jit(cholesky)/cholesky | solution.py:12
  456.7 0.6 compare_reduce_fusion
  457.3 0.7 fusion.7
  458.0 9.8 %custom-call.7 = f32[1,128,128]{1,2,0:T(8,128)S(1)} custom-call(f32[1,128,128]{2,1,0:T(8,128)S(1)} %fusion.7), custom_call_target="InvertDiagBlocksLowerTriangular" | custom-call | tf_op jit(solution)/shard_map/triangular_solve/custom-call.0 | solution.py:13
  467.8 0.4 fusion.8
  468.2 0.8 copy.27
  469.1 6.9 %fusion = f32[128,16,256]{2,0,1:T(8,128)S(1)} fusion(f32[512,16,256]{2,0,1:T(8,128)} %bitcast.50, f32[128,512]{1,0:T(8,128)S(1)} %fusion.8), kind=kOutput, calls=%fused_computation.1 | convolution fusion | flops 3221225472 | bytes 10747904 | tf_op jit(solution)/shard_map/mk,mbc->kbc/dot_general | solution.py:29
  476.0 2.5 copy.28
  (11 shorter events, 0.3 us)
Async XLA Ops:
  7.2 381.9 %copy-start = (f32[512,128]{1,0:T(8,128)S(1)}, f32[512,128]{1,0:T(8,128)}, u32[]{:S(2)}) copy-start(f32[512,128]{1,0:T(8,128)} %param.6) | copy-start | bytes 786436
  7.2 338.5 %reduce-scatter.2.cloned.1.call-start = ((), (), s32[]{:S(2)}) async-start(), calls=%async_computation.2 | async-start | bytes 1179648 | tf_op jit(solution)/shard_map/reduce_scatter | solution.py:24
  313.5 75.5 %all-reduce.2.cloned.1.call-start = ((), (), s32[]{:S(2)}) async-start(), calls=%async_computation.3 | async-start | bytes 262144 | tf_op jit(solution)/shard_map/psum | solution.py:25
Sparse Core Ops, SparseCore 0:
  313.6 32.0 reduce-scatter.1
  348.6 40.4 all-reduce.1
where the time goes:
time: 489 us; the launch traced here: 486 us
  blocking collectives  219 us (45%)
  local copies, waits for them, and re-layouts  90.7 us (19%)
  other arithmetic  72 us (15%)
  waiting for transfers between devices  62.7 us (13%)
  matrix products  26.3 us (5%)
  between operations  14.4 us (3%)
    all_to_all x1, blocking collectives, on_device(): lax.all_to_all(field_slab, 'fiber', split_axis=2, concat_axis=0, tiled=True)  191 us
    unnamed x8, local copies, waits for them, and re-layouts  61.4 us
    reduce_scatter x1, waiting for transfers between devices, on_device(): lax.psum_scatter(local_gram, 'fiber', scatter_dimension=0, tiled=True)  32.2 us
    psum x1, waiting for transfers between devices, on_device(): gram_share = lax.psum(fiber_share, 'group') / column_count  30.5 us
    all_to_all x3, local copies, waits for them, and re-layouts, on_device(): lax.all_to_all(field_slab, 'fiber', split_axis=2, concat_axis=0, tiled=True)  29.1 us
    all_gather x2, blocking collectives, on_device(): lax.all_gather(image_rows, 'fiber', axis=0, tiled=True)  28.7 us
    all_to_all x1, other arithmetic, on_device(): lax.all_to_all(field_slab, 'fiber', split_axis=2, concat_axis=0, tiled=True)  26.2 us
    another operation x6, other arithmetic, orthonormal(): cholesky_factor = jnp.linalg.cholesky(inner_products)  24.8 us
  transfers between devices with their start and end apart: 2, of which 2 were waited for; matrix products, arithmetic and copies ran while one was open for 3% of the time, Pallas kernels for 0%

commit v1 on v0

--- a/solution.py
+++ b/solution.py
@@ -22,7 +22,7 @@
     local_gram = jnp.dot(columns, columns.T, precision=precise)
     subspace = start_basis
     fiber_share = lax.psum_scatter(local_gram, "fiber", scatter_dimension=0, tiled=True)
-    gram_share = lax.psum(fiber_share, "group") / column_count
+    gram_share = jnp.sum(lax.all_gather(fiber_share, "group"), axis=0) / column_count
     for iteration in range(ITERS):
         image_rows = jnp.dot(gram_share, subspace, precision=precise)
         subspace = orthonormal(lax.all_gather(image_rows, "fiber", axis=0, tiled=True))

time: 489 us -> 454 us (0.928)
  waiting for transfers between devices: 62.7 us -> 19.6 us
  blocking collectives: 219 us -> 230 us
    psum x1 -> x0, waiting for transfers between devices: 30.5 us -> none  [on_device(): gram_share = lax.psum(fiber_share, 'group') / column_count]
    reduce_scatter x1, waiting for transfers between devices: 32.2 us -> 19.5 us  [on_device(): lax.psum_scatter(local_gram, 'fiber', scatter_dimension=0, tiled=True)]
    all_gather x0 -> x1, blocking collectives: none -> 10.3 us  [on_device(): lax.all_gather(fiber_share, 'group')]
  transfers between devices with their start and end apart: 2 -> 1, of which waited for: 2 -> 1; matrix products, arithmetic and copies ran while one was open for 3% -> 3% of each run, Pallas kernels for 0% -> 0%
where the time goes in v1:
time: 454 us; the launch traced here: 451 us
  blocking collectives  230 us (51%)
  local copies, waits for them, and re-layouts  90.3 us (20%)
  other arithmetic  72 us (16%)
  matrix products  24.4 us (5%)
  waiting for transfers between devices  19.6 us (4%)
  between operations  14.4 us (3%)
    all_to_all x1, blocking collectives, on_device(): lax.all_to_all(field_slab, 'fiber', split_axis=2, concat_axis=0, tiled=True)  191 us
    unnamed x8, local copies, waits for them, and re-layouts  61.4 us
    all_gather x2, blocking collectives, on_device(): lax.all_gather(image_rows, 'fiber', axis=0, tiled=True)  28.8 us
    all_to_all x3, local copies, waits for them, and re-layouts, on_device(): lax.all_to_all(field_slab, 'fiber', split_axis=2, concat_axis=0, tiled=True)  28.7 us
    all_to_all x1, other arithmetic, on_device(): lax.all_to_all(field_slab, 'fiber', split_axis=2, concat_axis=0, tiled=True)  26.2 us
    another operation x6, other arithmetic, orthonormal(): cholesky_factor = jnp.linalg.cholesky(inner_products)  24.8 us
    another operation x4, other arithmetic, orthonormal(): lax.linalg.triangular_solve(cholesky_factor, images, left_side=False, low...  20.9 us
    reduce_scatter x1, waiting for transfers between devices, on_device(): lax.psum_scatter(local_gram, 'fiber', scatter_dimension=0, tiled=True)  19.5 us
  transfers between devices with their start and end apart: 1, of which 1 were waited for; matrix products, arithmetic and copies ran while one was open for 3% of the time, Pallas kernels for 0%

profile of v1, /device:TPU:0, one launch (start us, length us, event | category | flops | bytes accessed | tf_op | source)
XLA Modules:
  0.0 450.7 jit_solution(11925346655807121087)
XLA Ops:
  7.2 15.6 %copy.22 = f32[64,16,2048]{0,1,2:T(8,128)} copy(f32[64,16,2048]{2,1,0:T(8,128)} %param.5) | data formatting | bytes 16777216 | tf_op args[0]
  22.8 15.4 %reshape.28 = f32[8,1,262144]{2,1,0:T(1,128)} reshape(f32[2048,16,64]{2,1,0:T(8,128)} %bitcast.50) | data formatting | bytes 16777216
  38.2 190.9 %all_to_all.18 = f32[8,1,262144]{2,1,0:T(1,128)} all-to-all(f32[8,1,262144]{2,1,0:T(1,128)} %reshape.28), channel_id=1, replica_groups=mesh['fiber'=8,'group'=4] {'fiber'}, dimensions={0} | all-to-all | bytes 16777216 | tf_op jit(solution)/shard_map/all_to_all | solution.py:20
  229.1 0.5 broadcast.36
  229.6 26.2 %reduce.4 = f32[8,262144]{1,0:T(8,128)} reduce(f32[8,1,262144]{2,1,0:T(1,128)} %all_to_all.18, f32[]{:T(128)} %broadcast.36), dimensions={1}, to_apply=%all_to_all.13.reduce_sub_computation | reduce | bytes 16777220 | tf_op jit(solution)/shard_map/all_to_all | solution.py:20
  255.8 15.6 %reshape.29 = f32[2048,16,64]{2,1,0:T(8,128)} reshape(f32[8,262144]{1,0:T(8,128)} %reduce.4) | data formatting | bytes 16777216
  271.4 15.4 %copy.23 = f32[64,16,8,256]{3,1,0,2:T(8,128)} copy(f32[64,16,8,256]{0,1,3,2:T(8,128)} %bitcast.48) | data formatting | bytes 16777216 | tf_op jit(solution)/shard_map/all_to_all | solution.py:20
  286.9 11.5 %copy.30 = f32[64,8,16,256]{3,1,2,0:T(8,128)S(1)} copy(f32[64,8,16,256]{3,2,1,0:T(8,128)} %bitcast.52) | data formatting | bytes 16777216
  298.4 14.7 %fusion.19 = f32[512,512]{1,0:T(8,128)} fusion(f32[512,4096]{1,0:T(8,128)S(1)} %bitcast.47), kind=kOutput, calls=%fused_computation.29 | convolution fusion | flops 12884901888 | bytes 9437184 | tf_op jit(solution)/shard_map/dot_general | solution.py:22
  313.1 12.8 %copy.26 = f32[8,64,16,256]{3,1,0,2:T(8,128)} copy(f32[8,64,16,256]{1,2,3,0:T(8,128)} %bitcast.49) | data formatting | bytes 16777216 | tf_op jit(solution)/shard_map/all_to_all | solution.py:20
  325.9 19.5 %reduce-scatter.2.cloned.1.call-done = f32[64,512]{1,0:T(8,128)} async-done(((f32[512,512]{1,0:T(8,128)}), f32[64,512]{1,0:T(8,128)}) %reduce-scatter.2.cloned.1.call-update) | async-done | bytes 131088 | tf_op jit(solution)/shard_map/reduce_scatter | solution.py:24
  345.4 10.3 %all-gather = f32[256,512]{1,0:T(8,128)S(1)} all-gather(f32[64,512]{1,0:T(8,128)} %reduce-scatter.2.cloned.1.call-done), channel_id=2, replica_groups=mesh['fiber'=8,'group'=4] {'group'}, dimensions={0}, use_global_device_ids=true | all-gather | bytes 655360 | tf_op jit(solution)/shard_map/all_gather | solution.py:25
  355.7 0.3 fusion.4
  356.0 14.4 %all_gather.14 = f32[512,128]{1,0:T(8,128)S(1)} all-gather(f32[64,128]{1,0:T(8,128)S(1)} %fusion.4), channel_id=1, replica_groups=mesh['fiber'=8,'group'=4] {'fiber'}, dimensions={0}, use_global_device_ids=true | all-gather | bytes 294912 | tf_op jit(solution)/shard_map/all_gather | solution.py:28
  370.4 0.6 fusion.20
  371.0 0.1 copy.24
  371.1 11.7 %cholesky.44 = f32[128,128]{1,0:T(8,128)S(1)} custom-call(f32[128,128]{1,0:T(8,128)S(1)} %fusion.12), custom_call_target="Cholesky" | custom-call | tf_op jit(solution)/shard_map/jit(cholesky)/cholesky | solution.py:12
  382.9 0.6 compare_reduce_fusion.1
  383.5 0.7 fusion.6
  384.2 9.8 %custom-call.6 = f32[1,128,128]{1,2,0:T(8,128)S(1)} custom-call(f32[1,128,128]{2,1,0:T(8,128)S(1)} %fusion.6), custom_call_target="InvertDiagBlocksLowerTriangular" | custom-call | tf_op jit(solution)/shard_map/triangular_solve/custom-call.0 | solution.py:13
  394.0 0.4 convolution_bitcast_fusion
  394.4 0.4 fusion.2
  394.8 14.4 %all_gather.15 = f32[512,128]{1,0:T(8,128)S(1)} all-gather(f32[64,128]{1,0:T(8,128)S(1)} %fusion.2), channel_id=1, replica_groups=mesh['fiber'=8,'group'=4] {'fiber'}, dimensions={0}, use_global_device_ids=true | all-gather | bytes 294912 | tf_op jit(solution)/shard_map/all_gather | solution.py:28
  409.3 0.6 fusion.21
  410.0 11.7 %cholesky.55 = f32[128,128]{1,0:T(8,128)S(1)} custom-call(f32[128,128]{1,0:T(8,128)S(1)} %fusion.10), custom_call_target="Cholesky" | custom-call | tf_op jit(solution)/shard_map/jit(cholesky)/cholesky | solution.py:12
  421.7 0.6 compare_reduce_fusion
  422.4 0.7 fusion.7
  423.0 9.8 %custom-call.7 = f32[1,128,128]{1,2,0:T(8,128)S(1)} custom-call(f32[1,128,128]{2,1,0:T(8,128)S(1)} %fusion.7), custom_call_target="InvertDiagBlocksLowerTriangular" | custom-call | tf_op jit(solution)/shard_map/triangular_solve/custom-call.0 | solution.py:13
  432.8 0.4 fusion.8
  433.3 0.8 copy.27
  434.1 6.9 %fusion = f32[128,16,256]{2,0,1:T(8,128)S(1)} fusion(f32[512,16,256]{2,0,1:T(8,128)} %bitcast.51, f32[128,512]{1,0:T(8,128)S(1)} %fusion.8), kind=kOutput, calls=%fused_computation.1 | convolution fusion | flops 3221225472 | bytes 10747904 | tf_op jit(solution)/shard_map/mk,mbc->kbc/dot_general | solution.py:29
  441.0 2.5 copy.28
  (10 shorter events, 0.3 us)
Async XLA Ops:
  7.2 348.6 %copy-start = (f32[512,128]{1,0:T(8,128)S(1)}, f32[512,128]{1,0:T(8,128)}, u32[]{:S(2)}) copy-start(f32[512,128]{1,0:T(8,128)} %param.6) | copy-start | bytes 786436
  7.2 338.2 %reduce-scatter.2.cloned.1.call-start = ((), (), s32[]{:S(2)}) async-start(), calls=%async_computation.2 | async-start | bytes 1179648 | tf_op jit(solution)/shard_map/reduce_scatter | solution.py:24
Sparse Core Ops, SparseCore 0:
  313.2 32.1 reduce-scatter.1
